TPU v7x, 32 devices: a whole 2x2x4 slice. The times are simulated.
32 devices in a mesh: sec: 4 (over z), harm: 8 (over y, x, core).
Axes of the slice: x: 2, y: 2, z: 4, core: 2. Of those that a mesh axis runs over, the one named last changes fastest.
Arguments:
- displacement: bfloat16 [12, 64, 32, 48, 128], P('sec', 'harm'), may hold values from -3 to 3
- stiffness: bfloat16 [32, 1536, 1536], P('harm'), may hold values from -0.15625 to 0.15625
- contact_limit: float32 [12, 32, 48], P('sec', None, 'harm'), may hold values from 1 to 12
- pair_list: int32 [72, 3], replicated, may hold values from 0 to 31, as said below
- pair_count: int32 [4], replicated, may hold values from 3 to 18, as said below
Outputs:
- residual: bfloat16 [12, 64, 32, 48, 128], P('sec', 'harm')
Inputs may be any that keep to these rules, and one draw needn't show every extreme that they name: `pair_list`: rows of index i of sec (the aligned blocks of 18 rows) have owners among sectors i * 3 to i * 3 + 2 and partners equal to owner + 1 or owner - 1 modulo 12; rows at or past that index's pair_count are unused and hold entries in range; among used rows of one index, at most 6 have partners on the same index, at most 6 on index i + 1 and at most 6 on index i - 1 (modulo the size of sec), and some index reaches 6 in all three groups in every draw. `pair_count`: every index of sec has at least one used row in each of its three groups; some index uses all its rows.
All inputs are finite; a program needn't handle non-finite values.
Results may differ from a plain program's by a relative error of at most 0.004.
Values may be sent and summed in bfloat16 or wider, within the bound.
No kernel may reach another device: no remote copies, remote signals or barrier semaphores. Data moves between devices by JAX's collectives and lax.ppermute only.
A program may use at most 192 MiB of HBM per device.

v0:
```python
import math
import jax
import jax.numpy as jnp
from jax import lax
from jax.sharding import PartitionSpec as P

NT = 128


def with_halo(cells, sides, width):
    for axis, dim in sides:
        count = lax.axis_size(axis)
        head = lax.slice_in_dim(cells, 0, width, axis=dim)
        tail = lax.slice_in_dim(cells, cells.shape[dim] - width, cells.shape[dim], axis=dim)
        cells = jnp.concatenate(
            [
                lax.ppermute(tail, axis, [(i, (i + 1) % count) for i in range(count)]),
                cells,
                lax.ppermute(head, axis, [((i + 1) % count, i) for i in range(count)]),
            ],
            axis=dim,
        )
    return cells


def tables(sample_count, coeff_count):
    n_index = jnp.arange(sample_count, dtype=jnp.int32)[:, None]
    c_index = jnp.arange(coeff_count, dtype=jnp.int32)[None, :]
    harmonic = c_index // 2 + 1
    phases = (harmonic * n_index % sample_count).astype(jnp.float32) * (
        2.0 * math.pi / sample_count
    )
    waveform = jnp.where(c_index % 2 == 0, jnp.cos(phases), jnp.sin(phases))
    return (waveform.astype(jnp.bfloat16), (waveform * (2.0 / sample_count)).astype(jnp.bfloat16))


def on_device(displacement, stiffness, contact_limit, pair_list, pair_count):
    sec_count = lax.axis_size("sec")
    sec_index = lax.axis_index("sec")
    harm_count = lax.axis_size("harm")
    sectors_here, coeffs_here, blocks_total, dofs_total, batch_cols = displacement.shape
    coeff_total = coeffs_here * harm_count
    forward_table, inverse_table = tables(NT, coeff_total)
    exchanged = lax.all_to_all(displacement, "harm", split_axis=3, concat_axis=1, tiled=True)
    waveform = jnp.einsum(
        "nc,scbdx->snbdx", forward_table, exchanged, preferred_element_type=jnp.float32
    )
    samples = waveform.astype(jnp.bfloat16)
    slots_dev = pair_list.shape[0] // sec_count
    capacity = slots_dev // 3
    sector_total = sectors_here * sec_count

    def bucket(device):
        rows = lax.dynamic_slice_in_dim(pair_list, device * slots_dev, slots_dev, 0)
        row_index = jnp.arange(slots_dev, dtype=jnp.int32)
        is_valid = row_index < pair_count[device]
        owners = rows[:, 0]
        partners = rows[:, 1]
        blocks = rows[:, 2]
        partner_dev = partners // sectors_here
        group = jnp.where(
            partner_dev == device, 0, jnp.where(partners == (owners + 1) % sector_total, 1, 2)
        )
        matches = (
            (group[:, None] == jnp.arange(3, dtype=jnp.int32)[None, :]) & is_valid[:, None]
        ).astype(jnp.int32)
        before = jnp.cumsum(matches, axis=0) - matches
        ranking = jnp.sum(before * matches, axis=1)
        slot_index = jnp.where(is_valid, group * capacity + ranking, slots_dev)
        source = jnp.zeros((slots_dev,), jnp.int32).at[slot_index].set(row_index, mode="drop")
        live = jnp.zeros((slots_dev,), jnp.int32).at[slot_index].set(1, mode="drop")
        return (
            owners[source] - device * sectors_here,
            partners[source] - partner_dev[source] * sectors_here,
            blocks[source],
            live > 0,
        )

    own_owner, own_partner, own_block, own_live = bucket(sec_index)
    prev_bucket = bucket((sec_index + sec_count - 1) % sec_count)
    next_bucket = bucket((sec_index + 1) % sec_count)
    send_order = jnp.concatenate(
        [
            jnp.arange(2 * capacity, 3 * capacity, dtype=jnp.int32),
            jnp.arange(capacity, 2 * capacity, dtype=jnp.int32),
        ]
    )
    send_owner = own_owner[send_order]
    send_block = own_block[send_order]
    send_live = own_live[send_order]
    outgoing = samples[send_owner, :, send_block]
    outgoing = jnp.where(send_live[:, None, None, None], outgoing, jnp.zeros_like(outgoing))
    padded = with_halo(outgoing.reshape((2, capacity) + outgoing.shape[1:]), (("sec", 0),), 1)
    remote_wave = jnp.concatenate([padded[0], padded[3]], axis=0)
    local_wave = samples[own_owner[:capacity], :, own_block[:capacity]]
    owner_wave = jnp.concatenate([local_wave, remote_wave], axis=0)
    partner_index = jnp.concatenate(
        [
            own_partner[:capacity],
            prev_bucket[1][capacity : 2 * capacity],
            next_bucket[1][2 * capacity :],
        ]
    )
    block_index = jnp.concatenate(
        [
            own_block[:capacity],
            prev_bucket[2][capacity : 2 * capacity],
            next_bucket[2][2 * capacity :],
        ]
    )
    live_rows = jnp.concatenate(
        [
            own_live[:capacity],
            prev_bucket[3][capacity : 2 * capacity],
            next_bucket[3][2 * capacity :],
        ]
    )
    partner_wave = samples[partner_index, :, block_index]
    limits = contact_limit[partner_index, block_index][:, None, :, None]
    relative = owner_wave.astype(jnp.float32) - partner_wave.astype(jnp.float32)
    friction = jnp.where(
        live_rows[:, None, None, None], limits * jnp.tanh(relative / limits), jnp.float32(0.0)
    ).astype(jnp.bfloat16)
    pair_coeffs = jnp.einsum(
        "nc,rndx->rcdx", inverse_table, friction, preferred_element_type=jnp.float32
    ).astype(jnp.bfloat16)
    force = jnp.zeros(
        (sectors_here, coeff_total, blocks_total, samples.shape[3], batch_cols), jnp.float32
    )
    force = force.at[partner_index, :, block_index].add(-pair_coeffs.astype(jnp.float32))
    force = force.at[own_owner[:capacity], :, own_block[:capacity]].add(
        pair_coeffs[:capacity].astype(jnp.float32)
    )
    remote_force = friction[capacity:]
    back = with_halo(remote_force.reshape((2, capacity) + remote_force.shape[1:]), (("sec", 0),), 1)
    returned_wave = jnp.concatenate([back[3], back[0]], axis=0)
    returned = jnp.einsum(
        "nc,rndx->rcdx", inverse_table, returned_wave, preferred_element_type=jnp.float32
    ).astype(jnp.bfloat16)
    force = force.at[own_owner[capacity:], :, own_block[capacity:]].add(
        returned.astype(jnp.float32)
    )
    force_coeffs = force.astype(jnp.bfloat16)
    returned_coeffs = lax.all_to_all(force_coeffs, "harm", split_axis=1, concat_axis=3, tiled=True)
    harmonics_here = stiffness.shape[0]
    paired = displacement.reshape(
        sectors_here, harmonics_here, 2, blocks_total * dofs_total, batch_cols
    )
    product = jnp.einsum("hij,shpjx->shpix", stiffness, paired, preferred_element_type=jnp.float32)
    result = product.reshape(displacement.shape) + returned_coeffs.astype(jnp.float32)
    return result.astype(jnp.bfloat16)


def solution(mesh):
    in_specs = (
        P("sec", "harm", None, None, None),
        P("harm", None, None),
        P("sec", None, "harm"),
        P(),
        P(),
    )
    out_specs = P("sec", "harm", None, None, None)
    return jax.shard_map(
        on_device, mesh=mesh, in_specs=in_specs, out_specs=out_specs, check_vma=False
    )
```

profile of v0, /device:TPU:0, one launch (start us, length us, event | category | flops | bytes accessed | tf_op | source)
XLA Modules:
  0.0 445.1 jit_solution(13424681273661140205)
XLA Ops:
  0.0 9.9 %copy.38 = bf16[3,8,32,48,128]{4,2,1,0,3:T(8,128)(2,1)} copy(bf16[3,8,32,48,128]{4,3,2,1,0:T(8,128)(2,1)} %param.5) | data formatting | bytes 18874368 | tf_op args[0]
  9.9 5.3 %all-to-all-start = ((bf16[3,8,32,48,128]{4,2,1,0,3:T(8,128)(2,1)}), bf16[3,8,32,48,128]{4,2,1,0,3:T(8,128)(2,1)}, u32[]{:S(2)}, u32[]{:S(2)}) async-start(bf16[3,8,32,48,128]{4,2,1,0,3:T(8,128)(2,1)} %copy.38), calls=%async_computation | async-start | bytes 18874368 | tf_op jit(solution)/shard_map/all_to_all | solution.py:44
  15.3 0.7 fusion.88
  15.9 0.6 iota_compare_fusion.4
  16.8 0.6 iota_compare_fusion.3
  17.7 0.6 fusion.58
  18.4 0.6 scatter_custom_fusion.1
  19.0 0.6 scatter_custom_fusion.4
  19.8 0.6 fusion.59
  20.4 0.6 scatter_custom_fusion.5
  21.1 0.6 scatter_custom_fusion.2
  21.7 0.7 iota_compare_fusion.5
  22.7 0.7 fusion.57
  23.4 0.6 scatter_custom_fusion.3
  24.1 0.6 scatter_custom_fusion
  24.8 0.7 gather_fusion.5
  25.5 0.7 gather_fusion.4
  26.2 0.7 gather_fusion.3
  26.9 0.7 gather_fusion.2
  27.6 0.7 gather_fusion.1
  28.3 0.7 gather_fusion
  29.0 0.7 gather_fusion.6
  29.7 0.7 gather_fusion.10
  30.5 0.7 gather_fusion.13
  31.2 0.7 gather_fusion.14
  31.9 0.7 gather_fusion.12
  32.7 88.4 %all-to-all-done = bf16[3,8,32,48,128]{4,2,1,0,3:T(8,128)(2,1)} async-done(((bf16[3,8,32,48,128]{4,2,1,0,3:T(8,128)(2,1)}), bf16[3,8,32,48,128]{4,2,1,0,3:T(8,128)(2,1)}, u32[]{:S(2)}, u32[]{:S(2)}) %all-to-all-start) | async-done | bytes 9437216 | tf_op jit(solution)/shard_map/all_to_all | solution.py:44
  121.1 12.1 %convert_bitcast_fusion.1 = bf16[3,128,32,6,128]{4,1,3,2,0:T(8,128)(2,1)} fusion(bf16[3,8,8,32,6,128]{5,3,2,0,4,1:T(8,128)(2,1)} %bitcast.35, s32[64]{0:T(128)S(1)} %fusion.44, pred[64]{0:T(512)(128)(4,1)S(1)} %fusion.43), kind=kOutput, calls=%fused_computation.31 | convolution fusion | flops 1217527808 | bytes 28311872 | tf_op jit(solution)/shard_map/nc,scbdx->snbdx/dot_general | solution.py:45
  133.2 7.4 %gather_fusion.15 = bf16[12,128,6,128]{3,1,2,0:T(8,128)(2,1)S(1)} fusion(bf16[3,128,32,6,128]{4,1,3,2,0:T(8,128)(2,1)} %convert_bitcast_fusion.1, s32[12]{0:T(128)S(1)} %fusion.55), kind=kCustom, calls=%fused_computation.15 | custom fusion | bytes 4718688 | tf_op jit(solution)/shard_map/gather | solution.py:91
  140.6 0.2 broadcast_select_fusion
  140.9 1.6 slice_bitcast_fusion.3
  142.5 2.4 collective-permute-start
  144.8 2.3 collective-permute-start.1
  147.2 0.7 gather_fusion.8
  147.9 0.7 gather_fusion.7
  149.0 0.6 fusion.86
  149.7 1.4 gather_fusion.9
  151.1 0.6 pad_add_fusion
  151.7 0.6 fusion.61
  152.3 7.8 %gather_fusion.16 = bf16[18,128,6,128]{3,1,2,0:T(8,128)(2,1)S(1)} fusion(bf16[3,128,32,6,128]{4,1,3,2,0:T(8,128)(2,1)} %convert_bitcast_fusion.1, s32[18]{0:T(128)S(1)} %get-tuple-element.5), kind=kCustom, calls=%fused_computation.16 | custom fusion | bytes 7078032 | tf_op jit(solution)/shard_map/gather | solution.py:118
  160.0 8.2 %gather_fusion.11 = bf16[6,128,6,128]{3,1,2,0:T(8,128)(2,1)} fusion(bf16[3,128,32,6,128]{4,1,3,2,0:T(8,128)(2,1)} %convert_bitcast_fusion.1, s32[6]{0:T(128)S(1)} %get-tuple-element.26), kind=kCustom, calls=%fused_computation.11 | custom fusion | bytes 2359344 | tf_op jit(solution)/shard_map/gather | solution.py:95
  168.2 5.8 %collective-permute-done = bf16[1,6,128,6,128]{4,2,3,1,0:T(8,128)(2,1)} collective-permute-done((bf16[1,6,128,6,128]{4,2,3,1,0:T(8,128)(2,1)}, bf16[1,6,128,6,128]{4,2,3,1,0:T(8,128)(2,1)}, u32[]{:S(2)}, u32[]{:S(2)}) %collective-permute-start) | collective-permute-done | bytes 1179680 | tf_op jit(solution)/shard_map/ppermute | solution.py:17
  174.0 21.1 %collective-permute-done.1 = bf16[1,6,128,6,128]{4,2,3,1,0:T(8,128)(2,1)} collective-permute-done((bf16[1,6,128,6,128]{4,2,3,1,0:T(8,128)(2,1)}, bf16[1,6,128,6,128]{4,2,3,1,0:T(8,128)(2,1)}, u32[]{:S(2)}, u32[]{:S(2)}) %collective-permute-start.1) | collective-permute-done | bytes 1179680 | tf_op jit(solution)/shard_map/ppermute | solution.py:19
  195.2 4.0 select_convert_fusion
  199.2 1.7 slice_bitcast_fusion.1
  201.0 2.1 collective-permute-start.2
  203.2 2.0 convert_negate_fusion
  205.2 8.9 %broadcast_in_dim.72 = f32[3,64,32,6,128]{4,1,3,2,0:T(8,128)} broadcast(f32[]{:T(128)} %constant.120.clone.1), dimensions={} | broadcast | bytes 18874372 | tf_op jit(solution)/shard_map/broadcast_in_dim | solution.py:127
  214.1 10.9 %scatter_fusion = f32[3,64,32,6,128]{4,1,3,2,0:T(8,128)} fusion(f32[3,64,32,6,128]{4,1,3,2,0:T(8,128)} %broadcast_in_dim.72, s32[18]{0:T(128)S(1)} %fusion.60, f32[18,64,6,128]{3,1,2,0:T(8,128)S(1)} %get-tuple-element.30), kind=kCustom, calls=%fused_computation.23 | custom fusion | flops 884736 | bytes 10616976 | tf_op jit(solution)/shard_map/scatter-add | solution.py:130
  224.9 1.2 slice_convert_fusion
  226.1 3.6 scatter_fusion.1
  229.8 24.3 %collective-permute-done.2 = bf16[1,6,128,6,128]{4,2,3,1,0:T(8,128)(2,1)} collective-permute-done((bf16[1,6,128,6,128]{4,2,3,1,0:T(8,128)(2,1)}, bf16[1,6,128,6,128]{4,2,3,1,0:T(8,128)(2,1)}, u32[]{:S(2)}, u32[]{:S(2)}) %collective-permute-start.2) | collective-permute-done | bytes 1179680 | tf_op jit(solution)/shard_map/ppermute | solution.py:19
  254.1 2.3 convert_bitcast_fusion.2
  256.4 7.0 %scatter_fusion.2 = f32[3,64,32,6,128]{4,1,3,2,0:T(8,128)} fusion(f32[3,64,32,6,128]{4,1,3,2,0:T(8,128)} %scatter_fusion.1, s32[12]{0:T(128)S(1)} %fusion.56, f32[12,64,6,128]{3,1,2,0:T(8,128)S(1)} %convert_bitcast_fusion.2), kind=kCustom, calls=%fused_computation.25 | custom fusion | flops 589824 | bytes 7077984 | tf_op jit(solution)/shard_map/scatter-add | solution.py:140
  263.4 10.4 %convert_element_type.97 = bf16[3,64,32,6,128]{4,1,3,2,0:T(8,128)(2,1)} convert(f32[3,64,32,6,128]{4,1,3,2,0:T(8,128)} %scatter_fusion.2) | non-fusion elementwise | flops 4718592 | bytes 28311552 | tf_op jit(solution)/shard_map/convert_element_type | solution.py:143
  273.8 13.3 %copy.41 = bf16[3,64,32,6,128]{4,2,3,0,1:T(8,128)(2,1)} copy(bf16[3,64,32,6,128]{4,1,3,2,0:T(8,128)(2,1)} %convert_element_type.97) | data formatting | bytes 18874368 | tf_op jit(solution)/shard_map/convert_element_type | solution.py:143
  287.1 5.4 %all-to-all-start.1 = ((bf16[3,64,32,6,128]{4,2,3,0,1:T(8,128)(2,1)}), bf16[3,64,32,6,128]{4,2,3,0,1:T(8,128)(2,1)}, u32[]{:S(2)}, u32[]{:S(2)}) async-start(bf16[3,64,32,6,128]{4,2,3,0,1:T(8,128)(2,1)} %copy.41), calls=%async_computation.1 | async-start | bytes 18874368 | tf_op jit(solution)/shard_map/all_to_all | solution.py:144
  292.5 25.0 %fusion.6 = f32[3,4,2,1536,128]{3,4,2,0,1:T(8,128)} fusion(bf16[4,1536,1536]{2,1,0:T(8,128)(2,1)} %param.6, bf16[3,4,2,1536,128]{4,3,2,1,0:T(8,128)(2,1)} %bitcast.179), kind=kOutput, calls=%fused_computation.35 | convolution fusion | flops 14495514624 | bytes 47185920 | tf_op jit(solution)/shard_map/hij,shpjx->shpix/dot_general | solution.py:149
  317.4 18.6 %copy.36 = f32[3,4,2,1536,128]{4,3,2,1,0:T(8,128)} copy(f32[3,4,2,1536,128]{3,4,2,0,1:T(8,128)} %fusion.6) | data formatting | bytes 37748736 | tf_op jit(solution)/shard_map/hij,shpjx->shpix/transpose | solution.py:149
  336.1 61.7 %all-to-all-done.1 = bf16[3,64,32,6,128]{4,2,3,0,1:T(8,128)(2,1)} async-done(((bf16[3,64,32,6,128]{4,2,3,0,1:T(8,128)(2,1)}), bf16[3,64,32,6,128]{4,2,3,0,1:T(8,128)(2,1)}, u32[]{:S(2)}, u32[]{:S(2)}) %all-to-all-start.1) | async-done | bytes 9437216 | tf_op jit(solution)/shard_map/all_to_all | solution.py:144
  397.8 10.1 %copy.42 = bf16[3,64,32,6,128]{4,2,3,1,0:T(8,128)(2,1)} copy(bf16[3,64,32,6,128]{4,2,3,0,1:T(8,128)(2,1)} %all-to-all-done.1) | data formatting | bytes 18874368 | tf_op jit(solution)/shard_map/all_to_all | solution.py:144
  407.9 12.9 %convert_bitcast_fusion = f32[3,8,32,8,6,128]{5,2,4,1,3,0:T(8,128)} fusion(bf16[3,8,8,32,6,128]{5,3,4,2,1,0:T(8,128)(2,1)} %bitcast.178), kind=kLoop, calls=%fused_computation.26 | loop fusion | flops 4718592 | bytes 28311552 | tf_op jit(solution)/shard_map/convert_element_type | solution.py:150
  420.7 8.2 %copy.43 = f32[3,8,32,8,6,128]{5,2,4,3,1,0:T(8,128)S(1)} copy(f32[3,8,32,8,6,128]{5,2,4,1,3,0:T(8,128)} %convert_bitcast_fusion) | data formatting | bytes 37748736 | tf_op jit(solution)/shard_map/convert_element_type | solution.py:150
  428.9 15.9 %fusion.2 = bf16[3,8,32,48,128]{4,3,2,1,0:T(8,128)(2,1)} fusion(f32[3,8,32,48,128]{4,3,2,1,0:T(8,128)} %bitcast.176, f32[3,8,32,48,128]{4,2,3,1,0:T(8,128)S(1)} %bitcast.177), kind=kLoop, calls=%fused_computation.30 | loop fusion | flops 9437184 | bytes 47185920 | tf_op jit(solution)/shard_map/convert_element_type | solution.py:151
  (70 shorter events, 1.9 us)
Async XLA Ops:
  9.9 5.3 %copy-start.8 = (s32[4]{0:T(128)S(1)}, s32[4]{0:T(128)}, u32[]{:S(2)}) copy-start(s32[4]{0:T(128)} %param.9) | copy-start | bytes 52
  9.9 6.7 %copy-start.1 = (s32[72,3]{0,1:T(4,128)S(1)}, s32[72,3]{0,1:T(4,128)}, u32[]{:S(2)}) copy-start(s32[72,3]{0,1:T(4,128)} %param.8) | copy-start | bytes 2596
  9.9 111.2 %all-to-all-start = ((bf16[3,8,32,48,128]{4,2,1,0,3:T(8,128)(2,1)}), bf16[3,8,32,48,128]{4,2,1,0,3:T(8,128)(2,1)}, u32[]{:S(2)}, u32[]{:S(2)}) async-start(bf16[3,8,32,48,128]{4,2,1,0,3:T(8,128)(2,1)} %copy.38), calls=%async_computation | async-start | bytes 18874368 | tf_op jit(solution)/shard_map/all_to_all | solution.py:44
  32.5 88.6 %copy-start.3 = (pred[64]{0:T(512)(128)(4,1)}, pred[64]{0:T(512)(128)(4,1)S(1)}, u32[]{:S(2)}) copy-start(pred[64]{0:T(512)(128)(4,1)S(1)} %fusion.43) | copy-start | bytes 196
  32.6 88.5 %copy-start.5 = (s32[64]{0:T(128)}, s32[64]{0:T(128)S(1)}, u32[]{:S(2)}) copy-start(s32[64]{0:T(128)S(1)} %fusion.44) | copy-start | bytes 772
  140.9 7.8 %copy-start.2 = (f32[3,32,6]{1,2,0:T(8,128)S(1)}, f32[3,32,6]{1,2,0:T(8,128)}, u32[]{:S(2)}) copy-start(f32[3,32,6]{1,2,0:T(8,128)} %param.7) | copy-start | bytes 6916
  142.5 31.6 %collective-permute-start = (bf16[1,6,128,6,128]{4,2,3,1,0:T(8,128)(2,1)}, bf16[1,6,128,6,128]{4,2,3,1,0:T(8,128)(2,1)}, u32[]{:S(2)}, u32[]{:S(2)}) collective-permute-start(bf16[1,6,128,6,128]{4,2,3,1,0:T(8,128)(2,1)} %get-tuple-element.10), channel_id=1, source_target_pairs={{0,8},{8,16},{16,24},{24,0},{1,9},{9,17},{17,25},{25,1},{2,10},{10... | collective-permute-start | bytes 3538952 | tf_op jit(solution)/shard_map/ppermute | solution.py:17
  144.8 50.3 %collective-permute-start.1 = (bf16[1,6,128,6,128]{4,2,3,1,0:T(8,128)(2,1)}, bf16[1,6,128,6,128]{4,2,3,1,0:T(8,128)(2,1)}, u32[]{:S(2)}, u32[]{:S(2)}) collective-permute-start(bf16[1,6,128,6,128]{4,2,3,1,0:T(8,128)(2,1)} %get-tuple-element.11), channel_id=1, source_target_pairs={{8,0},{16,8},{24,16},{0,24},{9,1},{17,9},{25,17},{1,25},{10,2},{18... | collective-permute-start | bytes 3538952 | tf_op jit(solution)/shard_map/ppermute | solution.py:19
  199.2 3.9 copy-start.9
  199.2 3.9 copy-start.10
  199.2 3.9 copy-start.4
  199.2 3.9 copy-start.6
  201.0 53.2 %collective-permute-start.2 = (bf16[1,6,128,6,128]{4,2,3,1,0:T(8,128)(2,1)}, bf16[1,6,128,6,128]{4,2,3,1,0:T(8,128)(2,1)}, u32[]{:S(2)}, u32[]{:S(2)}) collective-permute-start(bf16[1,6,128,6,128]{4,2,3,1,0:T(8,128)(2,1)} %get-tuple-element.8), channel_id=1, source_target_pairs={{8,0},{16,8},{24,16},{0,24},{9,1},{17,9},{25,17},{1,25},{10,2},{18... | collective-permute-start | bytes 3538952 | tf_op jit(solution)/shard_map/ppermute | solution.py:19
  203.0 51.1 %collective-permute-start.3 = (bf16[1,6,128,6,128]{4,2,3,1,0:T(8,128)(2,1)}, bf16[1,6,128,6,128]{4,2,3,1,0:T(8,128)(2,1)}, u32[]{:S(2)}, u32[]{:S(2)}) collective-permute-start(bf16[1,6,128,6,128]{4,2,3,1,0:T(8,128)(2,1)} %get-tuple-element.9), channel_id=1, source_target_pairs={{0,8},{8,16},{16,24},{24,0},{1,9},{9,17},{17,25},{25,1},{2,10},{10... | collective-permute-start | bytes 3538952 | tf_op jit(solution)/shard_map/ppermute | solution.py:17
  214.1 12.1 %copy-start = (s32[6]{0:T(128)S(1)}, s32[6]{0:T(128)}, u32[]{:S(2)}) copy-start(s32[6]{0:T(128)} %get-tuple-element.25) | copy-start | bytes 76
  224.9 29.2 %copy-start.7 = (s32[64]{0:T(128)S(1)}, s32[64]{0:T(128)}, u32[]{:S(2)}) copy-start(s32[64]{0:T(128)} %copy-done.5) | copy-start | bytes 772
  287.1 110.7 %all-to-all-start.1 = ((bf16[3,64,32,6,128]{4,2,3,0,1:T(8,128)(2,1)}), bf16[3,64,32,6,128]{4,2,3,0,1:T(8,128)(2,1)}, u32[]{:S(2)}, u32[]{:S(2)}) async-start(bf16[3,64,32,6,128]{4,2,3,0,1:T(8,128)(2,1)} %copy.41), calls=%async_computation.1 | async-start | bytes 18874368 | tf_op jit(solution)/shard_map/all_to_all | solution.py:144
where the time goes:
time: 453 us; the launch traced here: 445 us
  waiting for transfers between devices  201 us (44%)
  local copies, waits for them, and re-layouts  111 us (25%)
  other arithmetic  73 us (16%)
  matrix products  41.4 us (9%)
  starting transfers between devices  17.5 us (4%)
    all_to_all x1, waiting for transfers between devices, on_device(): lax.all_to_all(displacement, 'harm', split_axis=3, concat_axis=1, tiled=T...  88.4 us
    all_to_all x1, waiting for transfers between devices, on_device(): lax.all_to_all(force_coeffs, 'harm', split_axis=1, concat_axis=3, tiled=T...  61.7 us
    ppermute x2, waiting for transfers between devices, with_halo(): lax.ppermute(head, axis, [((i + 1) % count, i) for i in range(count)])  45.5 us
    dot_general x1, matrix products, on_device(): jnp.einsum('hij,shpjx->shpix', stiffness, paired, preferred_element_type=...  25 us
    transpose x1, local copies, waits for them, and re-layouts, on_device(): jnp.einsum('hij,shpjx->shpix', stiffness, paired, preferred_element_type=...  18.6 us
    convert_element_type x1, other arithmetic, on_device(): return result.astype(jnp.bfloat16)  15.9 us
    convert_element_type x1, local copies, waits for them, and re-layouts, on_device(): force_coeffs = force.astype(jnp.bfloat16)  13.3 us
    convert_element_type x1, other arithmetic, on_device(): returned_coeffs.astype(jnp.float32)  12.9 us
  transfers between devices with their start and end apart: 6, of which 5 were waited for; matrix products, arithmetic and copies ran while one was open for 24% of the time, Pallas kernels for 0%

commit v1 on v0

--- a/solution.py
+++ b/solution.py
@@ -141,7 +141,12 @@
         returned.astype(jnp.float32)
     )
     force_coeffs = force.astype(jnp.bfloat16)
-    returned_coeffs = lax.all_to_all(force_coeffs, "harm", split_axis=1, concat_axis=3, tiled=True)
+    returned_coeffs = jnp.concatenate(
+        lax.all_to_all(
+            jnp.stack(jnp.split(force_coeffs, lax.axis_size("harm"), axis=1)), "harm", 0, 0
+        ),
+        axis=3,
+    )
     harmonics_here = stiffness.shape[0]
     paired = displacement.reshape(
         sectors_here, harmonics_here, 2, blocks_total * dofs_total, batch_cols

time: 453 us -> 432 us (0.954); the launches traced: 445 us -> 431 us
  local copies, waits for them, and re-layouts: 111 us -> 103 us
  other arithmetic: 73 us -> 66.4 us
    ppermute x2, waiting for transfers between devices: 5.82 us -> 29.5 us  [with_halo(): lax.ppermute(tail, axis, [(i, (i + 1) % count) for i in range(count)])]
    ppermute x2, waiting for transfers between devices: 45.5 us -> 22 us  [with_halo(): lax.ppermute(head, axis, [((i + 1) % count, i) for i in range(count)])]
    convert_element_type x1 -> x0, local copies, waits for them, and re-layouts: 13.3 us -> none  [on_device(): force_coeffs = force.astype(jnp.bfloat16)]
    all_to_all x1 -> x0, local copies, waits for them, and re-layouts: 10.1 us -> none  [on_device(): lax.all_to_all(force_coeffs, 'harm', split_axis=1, concat_axis=3, tiled=T...]
    unnamed x24 -> x33, local copies, waits for them, and re-layouts: 10.1 us -> 19.4 us
    convert_element_type x1, local copies, waits for them, and re-layouts: 8.18 us -> 12.8 us  [on_device(): returned_coeffs.astype(jnp.float32)]
  transfers between devices with their start and end apart: 6 -> 6, of which waited for: 5 -> 6; matrix products, arithmetic and copies ran while one was open for 24% -> 25% of each run, Pallas kernels for 0% -> 0%
where the time goes in v1:
time: 432 us; the launch traced here: 431 us
  waiting for transfers between devices  202 us (47%)
  local copies, waits for them, and re-layouts  103 us (24%)
  other arithmetic  66.4 us (15%)
  matrix products  41.4 us (10%)
  starting transfers between devices  17.5 us (4%)
    all_to_all x1, waiting for transfers between devices, on_device(): lax.all_to_all(displacement, 'harm', split_axis=3, concat_axis=1, tiled=T...  88.4 us
    all_to_all x1, waiting for transfers between devices, on_device(): lax.all_to_all(jnp.stack(jnp.split(force_coeffs, lax.axis_size('harm'), a...  61.8 us
    ppermute x2, waiting for transfers between devices, with_halo(): lax.ppermute(tail, axis, [(i, (i + 1) % count) for i in range(count)])  29.5 us
    dot_general x1, matrix products, on_device(): jnp.einsum('hij,shpjx->shpix', stiffness, paired, preferred_element_type=...  25 us
    ppermute x2, waiting for transfers between devices, with_halo(): lax.ppermute(head, axis, [((i + 1) % count, i) for i in range(count)])  22 us
    unnamed x33, local copies, waits for them, and re-layouts  19.4 us
    transpose x1, local copies, waits for them, and re-layouts, on_device(): jnp.einsum('hij,shpjx->shpix', stiffness, paired, preferred_element_type=...  18.6 us
    convert_element_type x1, other arithmetic, on_device(): return result.astype(jnp.bfloat16)  13.1 us
  transfers between devices with their start and end apart: 6, of which 6 were waited for; matrix products, arithmetic and copies ran while one was open for 25% of the time, Pallas kernels for 0%

profile of v1, /device:TPU:0, one launch (start us, length us, event | category | flops | bytes accessed | tf_op | source)
XLA Modules:
  0.0 430.5 jit_solution(8961034495386462939)
XLA Ops:
  0.0 9.9 %copy.19 = bf16[3,8,32,48,128]{4,2,1,0,3:T(8,128)(2,1)} copy(bf16[3,8,32,48,128]{4,3,2,1,0:T(8,128)(2,1)} %param.5) | data formatting | bytes 18874368 | tf_op args[0]
  9.9 5.3 %all-to-all-start = ((bf16[3,8,32,48,128]{4,2,1,0,3:T(8,128)(2,1)}), bf16[3,8,32,48,128]{4,2,1,0,3:T(8,128)(2,1)}, u32[]{:S(2)}, u32[]{:S(2)}) async-start(bf16[3,8,32,48,128]{4,2,1,0,3:T(8,128)(2,1)} %copy.19), calls=%async_computation | async-start | bytes 18874368 | tf_op jit(solution)/shard_map/all_to_all | solution.py:44
  15.3 0.7 fusion.96
  15.9 0.6 iota_compare_fusion.4
  17.7 0.6 fusion.66
  18.4 0.6 scatter_custom_fusion.1
  19.0 0.6 scatter_custom_fusion.4
  20.4 0.6 scatter_custom_fusion.5
  21.7 0.7 iota_compare_fusion.5
  22.7 0.7 fusion.65
  23.4 0.6 scatter_custom_fusion.3
  24.8 0.7 gather_fusion.5
  25.5 0.7 gather_fusion.4
  26.2 0.7 gather_fusion.3
  26.9 0.7 gather_fusion.2
  27.6 0.7 gather_fusion.1
  28.3 0.7 gather_fusion
  29.0 0.7 gather_fusion.6
  29.7 0.7 gather_fusion.10
  30.5 0.7 gather_fusion.13
  31.2 0.7 gather_fusion.14
  31.9 0.7 gather_fusion.12
  32.7 88.4 %all-to-all-done = bf16[3,8,32,48,128]{4,2,1,0,3:T(8,128)(2,1)} async-done(((bf16[3,8,32,48,128]{4,2,1,0,3:T(8,128)(2,1)}), bf16[3,8,32,48,128]{4,2,1,0,3:T(8,128)(2,1)}, u32[]{:S(2)}, u32[]{:S(2)}) %all-to-all-start) | async-done | bytes 9437216 | tf_op jit(solution)/shard_map/all_to_all | solution.py:44
  121.1 12.1 %convert_bitcast_fusion.1 = bf16[3,128,32,6,128]{4,1,3,2,0:T(8,128)(2,1)} fusion(bf16[3,8,8,32,6,128]{5,3,2,0,4,1:T(8,128)(2,1)} %bitcast.35, s32[64]{0:T(128)S(1)} %fusion.52, pred[64]{0:T(512)(128)(4,1)S(1)} %fusion.51), kind=kOutput, calls=%fused_computation.31 | convolution fusion | flops 1217527808 | bytes 28311872 | tf_op jit(solution)/shard_map/nc,scbdx->snbdx/dot_general | solution.py:45
  133.2 7.4 %gather_fusion.15 = bf16[12,128,6,128]{3,1,2,0:T(8,128)(2,1)S(1)} fusion(bf16[3,128,32,6,128]{4,1,3,2,0:T(8,128)(2,1)} %convert_bitcast_fusion.1, s32[12]{0:T(128)S(1)} %fusion.63), kind=kCustom, calls=%fused_computation.15 | custom fusion | bytes 4718688 | tf_op jit(solution)/shard_map/gather | solution.py:91
  140.9 1.6 slice_bitcast_fusion.11
  142.5 2.4 collective-permute-start
  144.8 2.1 collective-permute-start.1
  147.0 0.7 gather_fusion.8
  147.7 0.7 gather_fusion.7
  148.8 0.6 fusion.94
  149.4 1.4 gather_fusion.9
  152.0 7.8 %gather_fusion.16 = bf16[18,128,6,128]{3,1,2,0:T(8,128)(2,1)S(1)} fusion(bf16[3,128,32,6,128]{4,1,3,2,0:T(8,128)(2,1)} %convert_bitcast_fusion.1, s32[18]{0:T(128)S(1)} %get-tuple-element.5), kind=kCustom, calls=%fused_computation.16 | custom fusion | bytes 7078032 | tf_op jit(solution)/shard_map/gather | solution.py:118
  159.8 8.2 %gather_fusion.11 = bf16[6,128,6,128]{3,1,2,0:T(8,128)(2,1)} fusion(bf16[3,128,32,6,128]{4,1,3,2,0:T(8,128)(2,1)} %convert_bitcast_fusion.1, s32[6]{0:T(128)S(1)} %get-tuple-element.26), kind=kCustom, calls=%fused_computation.11 | custom fusion | bytes 2359344 | tf_op jit(solution)/shard_map/gather | solution.py:95
  167.9 6.1 %collective-permute-done = bf16[1,6,128,6,128]{4,2,3,1,0:T(8,128)(2,1)} collective-permute-done((bf16[1,6,128,6,128]{4,2,3,1,0:T(8,128)(2,1)}, bf16[1,6,128,6,128]{4,2,3,1,0:T(8,128)(2,1)}, u32[]{:S(2)}, u32[]{:S(2)}) %collective-permute-start) | collective-permute-done | bytes 1179680 | tf_op jit(solution)/shard_map/ppermute | solution.py:17
  174.0 20.9 %collective-permute-done.1 = bf16[1,6,128,6,128]{4,2,3,1,0:T(8,128)(2,1)} collective-permute-done((bf16[1,6,128,6,128]{4,2,3,1,0:T(8,128)(2,1)}, bf16[1,6,128,6,128]{4,2,3,1,0:T(8,128)(2,1)}, u32[]{:S(2)}, u32[]{:S(2)}) %collective-permute-start.1) | collective-permute-done | bytes 1179680 | tf_op jit(solution)/shard_map/ppermute | solution.py:19
  194.9 4.0 select_convert_fusion
  199.0 1.7 slice_bitcast_fusion.9
  200.7 2.3 collective-permute-start.2
  203.2 2.0 convert_negate_fusion
  205.2 8.9 %broadcast_in_dim.72 = f32[3,64,32,6,128]{4,1,3,2,0:T(8,128)} broadcast(f32[]{:T(128)} %constant.120.clone.1), dimensions={} | broadcast | bytes 18874372 | tf_op jit(solution)/shard_map/broadcast_in_dim | solution.py:127
  214.1 10.3 %scatter_fusion = f32[3,64,32,6,128]{4,1,3,2,0:T(8,128)} fusion(f32[3,64,32,6,128]{4,1,3,2,0:T(8,128)} %broadcast_in_dim.72, s32[18]{0:T(128)S(1)} %fusion.68, f32[18,64,6,128]{3,1,2,0:T(8,128)S(1)} %get-tuple-element.30), kind=kCustom, calls=%fused_computation.23 | custom fusion | flops 884736 | bytes 10616976 | tf_op jit(solution)/shard_map/scatter-add | solution.py:130
  224.4 1.2 slice_convert_fusion
  225.6 3.6 scatter_fusion.1
  229.3 1.1 collective-permute-done.2
  230.4 23.4 %collective-permute-done.3 = bf16[1,6,128,6,128]{4,2,3,1,0:T(8,128)(2,1)} collective-permute-done((bf16[1,6,128,6,128]{4,2,3,1,0:T(8,128)(2,1)}, bf16[1,6,128,6,128]{4,2,3,1,0:T(8,128)(2,1)}, u32[]{:S(2)}, u32[]{:S(2)}) %collective-permute-start.3) | collective-permute-done | bytes 1179680 | tf_op jit(solution)/shard_map/ppermute | solution.py:17
  253.8 2.3 convert_bitcast_fusion.2
  256.1 7.0 %scatter_fusion.2 = f32[3,64,32,6,128]{4,1,3,2,0:T(8,128)} fusion(f32[3,64,32,6,128]{4,1,3,2,0:T(8,128)} %scatter_fusion.1, s32[12]{0:T(128)S(1)} %fusion.64, f32[12,64,6,128]{3,1,2,0:T(8,128)S(1)} %convert_bitcast_fusion.2), kind=kCustom, calls=%fused_computation.25 | custom fusion | flops 589824 | bytes 7077984 | tf_op jit(solution)/shard_map/scatter-add | solution.py:140
  263.1 7.6 %convert_element_type.94 = bf16[3,64,32,6,128]{4,1,3,2,0:T(8,128)(2,1)S(1)} convert(f32[3,64,32,6,128]{4,1,3,2,0:T(8,128)} %scatter_fusion.2) | non-fusion elementwise | flops 4718592 | bytes 28311552 | tf_op jit(solution)/shard_map/convert_element_type | solution.py:143
  270.7 1.3 fusion.27
  272.1 1.3 fusion.26
  273.4 1.3 fusion.25
  274.7 1.3 fusion.24
  276.1 1.3 fusion.23
  277.4 1.3 fusion.22
  278.7 1.3 fusion.21
  280.1 1.3 fusion.20
  281.4 5.4 %all-to-all-start.1 = ((bf16[8,3,8,32,6,128]{5,2,4,3,1,0:T(8,128)(2,1)}), bf16[8,3,8,32,6,128]{5,2,4,3,1,0:T(8,128)(2,1)}, u32[]{:S(2)}, u32[]{:S(2)}) async-start(bf16[8,3,8,32,6,128]{5,2,4,3,1,0:T(8,128)(2,1)} %fusion.20), calls=%async_computation.1 | async-start | bytes 18874368 | tf_op jit(solution)/shard_map/all_to_all | solution.py:145
  286.8 25.0 %fusion.6 = f32[3,4,2,1536,128]{3,4,2,0,1:T(8,128)} fusion(bf16[4,1536,1536]{2,1,0:T(8,128)(2,1)} %param.6, bf16[3,4,2,1536,128]{4,3,2,1,0:T(8,128)(2,1)} %bitcast.208), kind=kOutput, calls=%fused_computation.35 | convolution fusion | flops 14495514624 | bytes 47185920 | tf_op jit(solution)/shard_map/hij,shpjx->shpix/dot_general | solution.py:154
  311.8 18.6 %copy.17 = f32[3,4,2,1536,128]{4,3,2,1,0:T(8,128)} copy(f32[3,4,2,1536,128]{3,4,2,0,1:T(8,128)} %fusion.6) | data formatting | bytes 37748736 | tf_op jit(solution)/shard_map/hij,shpjx->shpix/transpose | solution.py:154
  330.4 61.8 %all-to-all-done.1 = bf16[8,3,8,32,6,128]{5,2,4,3,1,0:T(8,128)(2,1)} async-done(((bf16[8,3,8,32,6,128]{5,2,4,3,1,0:T(8,128)(2,1)}), bf16[8,3,8,32,6,128]{5,2,4,3,1,0:T(8,128)(2,1)}, u32[]{:S(2)}, u32[]{:S(2)}) %all-to-all-start.1) | async-done | bytes 9437216 | tf_op jit(solution)/shard_map/all_to_all | solution.py:145
  392.2 12.4 %convert_bitcast_fusion = f32[3,8,32,8,6,128]{5,1,4,2,0,3:T(8,128)} fusion(bf16[8,3,8,32,6,128]{5,2,4,3,1,0:T(8,128)(2,1)} %all-to-all-done.1), kind=kLoop, calls=%fused_computation.30 | loop fusion | flops 4718592 | bytes 28311552 | tf_op jit(solution)/shard_map/convert_element_type | solution.py:155
  404.6 12.8 %copy.22 = f32[3,8,32,8,6,128]{5,2,4,3,1,0:T(8,128)S(1)} copy(f32[3,8,32,8,6,128]{5,1,4,2,0,3:T(8,128)} %convert_bitcast_fusion) | data formatting | bytes 37748736 | tf_op jit(solution)/shard_map/convert_element_type | solution.py:155
  417.4 13.1 %fusion.2 = bf16[3,8,32,48,128]{4,3,2,1,0:T(8,128)(2,1)} fusion(f32[3,8,32,48,128]{4,3,2,1,0:T(8,128)S(1)} %bitcast.206, f32[3,8,32,48,128]{4,2,3,1,0:T(8,128)S(1)} %bitcast.207), kind=kLoop, calls=%fused_computation.29 | loop fusion | flops 9437184 | bytes 47185920 | tf_op jit(solution)/shard_map/convert_element_type | solution.py:156
  (78 shorter events, 5.7 us)
Async XLA Ops:
  9.9 5.3 %copy-start.9 = (s32[4]{0:T(128)S(1)}, s32[4]{0:T(128)}, u32[]{:S(2)}) copy-start(s32[4]{0:T(128)} %param.9) | copy-start | bytes 52
  9.9 6.7 %copy-start.2 = (s32[72,3]{0,1:T(4,128)S(1)}, s32[72,3]{0,1:T(4,128)}, u32[]{:S(2)}) copy-start(s32[72,3]{0,1:T(4,128)} %param.8) | copy-start | bytes 2596
  9.9 111.2 %all-to-all-start = ((bf16[3,8,32,48,128]{4,2,1,0,3:T(8,128)(2,1)}), bf16[3,8,32,48,128]{4,2,1,0,3:T(8,128)(2,1)}, u32[]{:S(2)}, u32[]{:S(2)}) async-start(bf16[3,8,32,48,128]{4,2,1,0,3:T(8,128)(2,1)} %copy.19), calls=%async_computation | async-start | bytes 18874368 | tf_op jit(solution)/shard_map/all_to_all | solution.py:44
  32.5 88.6 %copy-start.4 = (pred[64]{0:T(512)(128)(4,1)}, pred[64]{0:T(512)(128)(4,1)S(1)}, u32[]{:S(2)}) copy-start(pred[64]{0:T(512)(128)(4,1)S(1)} %fusion.51) | copy-start | bytes 196
  32.6 88.5 %copy-start.7 = (s32[64]{0:T(128)}, s32[64]{0:T(128)S(1)}, u32[]{:S(2)}) copy-start(s32[64]{0:T(128)S(1)} %fusion.52) | copy-start | bytes 772
  133.2 15.2 %copy-start.3 = (f32[3,32,6]{1,2,0:T(8,128)S(1)}, f32[3,32,6]{1,2,0:T(8,128)}, u32[]{:S(2)}) copy-start(f32[3,32,6]{1,2,0:T(8,128)} %param.7) | copy-start | bytes 6916
  142.5 31.6 %collective-permute-start = (bf16[1,6,128,6,128]{4,2,3,1,0:T(8,128)(2,1)}, bf16[1,6,128,6,128]{4,2,3,1,0:T(8,128)(2,1)}, u32[]{:S(2)}, u32[]{:S(2)}) collective-permute-start(bf16[1,6,128,6,128]{4,2,3,1,0:T(8,128)(2,1)} %get-tuple-element.10), channel_id=1, source_target_pairs={{0,8},{8,16},{16,24},{24,0},{1,9},{9,17},{17,25},{25,1},{2,10},{10... | collective-permute-start | bytes 3538952 | tf_op jit(solution)/shard_map/ppermute | solution.py:17
  144.8 50.1 %collective-permute-start.1 = (bf16[1,6,128,6,128]{4,2,3,1,0:T(8,128)(2,1)}, bf16[1,6,128,6,128]{4,2,3,1,0:T(8,128)(2,1)}, u32[]{:S(2)}, u32[]{:S(2)}) collective-permute-start(bf16[1,6,128,6,128]{4,2,3,1,0:T(8,128)(2,1)} %get-tuple-element.11), channel_id=1, source_target_pairs={{8,0},{16,8},{24,16},{0,24},{9,1},{17,9},{25,17},{1,25},{10,2},{18... | collective-permute-start | bytes 3538952 | tf_op jit(solution)/shard_map/ppermute | solution.py:19
  194.9 8.2 %copy-start.10 = (s32[18,1]{0,1:T(1,128)S(1)}, s32[18,1]{0,1:T(1,128)}, u32[]{:S(2)}) copy-start(s32[18,1]{0,1:T(1,128)} %get-tuple-element.6) | copy-start | bytes 220
  194.9 8.2 %copy-start.11 = (s32[18,1]{0,1:T(1,128)S(1)}, s32[18,1]{0,1:T(1,128)}, u32[]{:S(2)}) copy-start(s32[18,1]{0,1:T(1,128)} %get-tuple-element.7) | copy-start | bytes 220
  194.9 8.2 %copy-start.5 = (pred[64]{0:T(512)(128)(4,1)S(1)}, pred[64]{0:T(512)(128)(4,1)}, u32[]{:S(2)}) copy-start(pred[64]{0:T(512)(128)(4,1)} %copy-done.4) | copy-start | bytes 196
  194.9 8.2 %copy-start.8 = (s32[64]{0:T(128)S(1)}, s32[64]{0:T(128)}, u32[]{:S(2)}) copy-start(s32[64]{0:T(128)} %copy-done.7) | copy-start | bytes 772
  200.7 29.7 %collective-permute-start.2 = (bf16[1,6,128,6,128]{4,2,3,1,0:T(8,128)(2,1)}, bf16[1,6,128,6,128]{4,2,3,1,0:T(8,128)(2,1)}, u32[]{:S(2)}, u32[]{:S(2)}) collective-permute-start(bf16[1,6,128,6,128]{4,2,3,1,0:T(8,128)(2,1)} %get-tuple-element.8), channel_id=1, source_target_pairs={{8,0},{16,8},{24,16},{0,24},{9,1},{17,9},{25,17},{1,25},{10,2},{18... | collective-permute-start | bytes 3538952 | tf_op jit(solution)/shard_map/ppermute | solution.py:19
  203.0 50.8 %collective-permute-start.3 = (bf16[1,6,128,6,128]{4,2,3,1,0:T(8,128)(2,1)}, bf16[1,6,128,6,128]{4,2,3,1,0:T(8,128)(2,1)}, u32[]{:S(2)}, u32[]{:S(2)}) collective-permute-start(bf16[1,6,128,6,128]{4,2,3,1,0:T(8,128)(2,1)} %get-tuple-element.9), channel_id=1, source_target_pairs={{0,8},{8,16},{16,24},{24,0},{1,9},{9,17},{17,25},{25,1},{2,10},{10... | collective-permute-start | bytes 3538952 | tf_op jit(solution)/shard_map/ppermute | solution.py:17
  214.1 11.5 %copy-start.1 = (s32[6]{0:T(128)S(1)}, s32[6]{0:T(128)}, u32[]{:S(2)}) copy-start(s32[6]{0:T(128)} %get-tuple-element.25) | copy-start | bytes 76
  214.1 39.8 %copy-start.6 = (pred[64]{0:T(512)(128)(4,1)S(1)}, pred[64]{0:T(512)(128)(4,1)}, u32[]{:S(2)}) copy-start(pred[64]{0:T(512)(128)(4,1)} %copy-done.4) | copy-start | bytes 196
  281.4 110.8 %all-to-all-start.1 = ((bf16[8,3,8,32,6,128]{5,2,4,3,1,0:T(8,128)(2,1)}), bf16[8,3,8,32,6,128]{5,2,4,3,1,0:T(8,128)(2,1)}, u32[]{:S(2)}, u32[]{:S(2)}) async-start(bf16[8,3,8,32,6,128]{5,2,4,3,1,0:T(8,128)(2,1)} %fusion.20), calls=%async_computation.1 | async-start | bytes 18874368 | tf_op jit(solution)/shard_map/all_to_all | solution.py:145
  404.6 12.8 %copy-start = (f32[3,4,2,1536,128]{4,3,2,1,0:T(8,128)S(1)}, f32[3,4,2,1536,128]{4,3,2,1,0:T(8,128)}, u32[]{:S(2)}) copy-start(f32[3,4,2,1536,128]{4,3,2,1,0:T(8,128)} %copy.17) | copy-start | bytes 56623108
